TPU v7x, 32 devices: a whole 2x2x4 slice. The times are simulated.
32 devices in a mesh: row: 4 (over z), col: 8 (over y, x, core).
Axes of the slice: x: 2, y: 2, z: 4, core: 2. Of those that a mesh axis runs over, the one named last changes fastest.
Arguments:
- a_matrix: float32 [16384, 16384], P('row', 'col'), may hold values from -2.25 to 2.25
- b_matrix: float32 [16384, 16384], P('row', 'col'), may hold values from -0.1 to 3.1
- x_block: float32 [16384, 64], P('row'), may hold values from -6 to 6
- r_block: float32 [16384, 64], P('row'), may hold values from -6 to 6
- p_block: float32 [16384, 64], P('row'), may hold values from -6 to 6
Outputs:
- x_next: float32 [16384, 64], P('row')
- r_next: float32 [16384, 64], P('row')
- p_next: float32 [16384, 64], P('row')
All inputs are finite; a program needn't handle non-finite values.
Results may differ from a plain program's by a relative error of at most 0.0003.
Values sent between devices are 32-bit elements; how exact they have to be, the bound alone decides.
A program may use at most 192 MiB of HBM per device.

v0:
```python
import math
import jax
import jax.numpy as jnp
from jax import lax
from jax.sharding import PartitionSpec as P

N = 16384
ITERS = 2
NS_STEPS = 8


def spread(value, axis, source):
    kept = jnp.where(lax.axis_index(axis) == source, value, 0).astype(value.dtype)
    return lax.psum(kept, axis)


def matmul(left, right):
    return jnp.dot(left, right, precision=lax.Precision.HIGHEST, preferred_element_type=jnp.float32)


def ritz_step(gram_a, gram_b, count):
    gram_a = 0.5 * (gram_a + gram_a.T)
    gram_b = 0.5 * (gram_b + gram_b.T)
    lower = jnp.linalg.cholesky(gram_b)
    half = lax.linalg.triangular_solve(lower, gram_a, left_side=True, lower=True)
    middle = lax.linalg.triangular_solve(lower, half.T, left_side=True, lower=True)
    middle = 0.5 * (middle + middle.T)
    extent = middle.shape[0]
    ident = jnp.eye(extent, dtype=middle.dtype)
    shift = jnp.trace(middle) / extent
    centred = middle - shift * ident
    sign_est = centred / jnp.sqrt(jnp.sum(centred * centred) + 1e-06)
    for turn in range(NS_STEPS):
        sign_est = 1.5 * sign_est - 0.5 * matmul(sign_est, matmul(sign_est, sign_est))
    filtered = (0.5 * (ident - sign_est))[:, :count]
    coords = lax.linalg.triangular_solve(
        lower, filtered, left_side=True, lower=True, transpose_a=True
    ) * math.sqrt(N)
    reduced = matmul(filtered.T, matmul(middle, filtered))
    return (coords, reduced)


def local(a_matrix, b_matrix, x_block, r_block, p_block):
    ratio = lax.axis_size("col") // lax.axis_size("row")
    col_index = lax.axis_index("col")
    tile_cols = a_matrix.shape[1]
    width = x_block.shape[1]
    for turn in range(ITERS):
        panel = jnp.concatenate([x_block, r_block, p_block], axis=1)
        own_part = lax.dynamic_slice_in_dim(panel, col_index % ratio * tile_cols, tile_cols, 0)
        matched = spread(own_part, "row", col_index // ratio)
        products = lax.psum(
            jnp.concatenate([matmul(a_matrix, matched), matmul(b_matrix, matched)], axis=1), "col"
        )
        grams = lax.psum(matmul(panel.T, products), "row")
        coords, reduced = ritz_step(grams[:, : 3 * width], grams[:, 3 * width :], width)
        new_resid = matmul(products[:, : 3 * width], coords) - matmul(
            matmul(products[:, 3 * width :], coords), reduced
        )
        x_block = matmul(panel, coords)
        p_block = matmul(panel[:, width:], coords[width:])
        r_block = new_resid
    return (x_block, r_block, p_block)


def solution(mesh):
    return jax.shard_map(
        local,
        mesh=mesh,
        in_specs=(P("row", "col"), P("row", "col"), P("row", None), P("row", None), P("row", None)),
        out_specs=(P("row", None), P("row", None), P("row", None)),
        check_vma=False,
    )
```

profile of v0, /device:TPU:0, one launch (start us, length us, event | category | flops | bytes accessed | tf_op | source)
XLA Modules:
  0.0 861.8 jit_solution(8819377317058890777)
XLA Ops:
  12.5 71.8 %all-reduce.12.cloned.1.call-done = f32[2048,192]{0,1:T(8,128)} async-done(((f32[2048,192]{0,1:T(8,128)}), f32[2048,192]{0,1:T(8,128)}) %all-reduce.12.cloned.1.call-update) | async-done | bytes 1572880 | tf_op jit(solution)/shard_map/psum | solution.py:14
  84.3 40.1 %convolution_bitcast_fusion.2 = f32[4096,192]{0,1:T(8,128)S(1)} fusion(f32[2048,192]{0,1:T(8,128)} %all-reduce.12.cloned.1.call-done, f32[4096,2048]{1,0:T(8,128)} %param.11), kind=kOutput, calls=%fused_computation.4 | convolution fusion | flops 19327352832 | bytes 38273024 | tf_op jit(solution)/shard_map/dot_general | solution.py:18
  124.4 37.8 %convolution_bitcast_fusion.3 = f32[4096,192]{0,1:T(8,128)S(1)} fusion(f32[2048,192]{0,1:T(8,128)S(1)} %copy-done.2, f32[4096,2048]{1,0:T(8,128)} %param.10), kind=kOutput, calls=%fused_computation.5 | convolution fusion | flops 19327352832 | bytes 38273024 | tf_op jit(solution)/shard_map/dot_general | solution.py:18
  162.2 3.1 pad_maximum_fusion
  165.3 103.2 %all-reduce.14.cloned.1.call-done = f32[4096,384]{0,1:T(8,128)} async-done(((f32[4096,384]{0,1:T(8,128)}), f32[4096,384]{0,1:T(8,128)}) %all-reduce.14.cloned.1.call-update) | async-done | bytes 6291472 | tf_op jit(solution)/shard_map/psum | solution.py:52
  268.5 9.2 %fusion.104 = f32[192,384]{1,0:T(8,128)} fusion(f32[4096,192]{0,1:T(8,128)S(1)} %constant_dynamic-update-slice_fusion, f32[4096,384]{0,1:T(8,128)} %all-reduce.14.cloned.1.call-done), kind=kOutput, calls=%fused_computation.191 | convolution fusion | flops 3623878656 | bytes 9732096 | tf_op jit(solution)/shard_map/dot_general | solution.py:18
  278.0 35.9 %all-reduce.16.cloned.1.call-done = f32[192,384]{1,0:T(8,128)} async-done(((f32[192,384]{1,0:T(8,128)}), f32[192,384]{1,0:T(8,128)}) %all-reduce.16.cloned.1.call-update) | async-done | bytes 294928 | tf_op jit(solution)/shard_map/psum | solution.py:55
  313.9 1.8 slice.231
  315.7 1.7 copy.8
  317.4 1.9 fusion.42
  319.3 1.7 copy.10
  323.4 1.6 copy.11
  325.0 13.2 %cholesky.136 = f32[128,128]{1,0:T(8,128)} custom-call(f32[128,128]{1,0:T(8,128)} %copy.11), custom_call_target="Cholesky" | custom-call | tf_op jit(solution)/shard_map/jit(cholesky)/cholesky | solution.py:24
  341.2 11.3 %custom-call.19 = f32[1,128,128]{1,2,0:T(8,128)} custom-call(f32[1,128,128]{2,1,0:T(8,128)} %get-tuple-element.81), custom_call_target="InvertDiagBlocksLowerTriangular" | custom-call | tf_op jit(solution)/shard_map/jit(cholesky)/cholesky | solution.py:24
  352.4 1.8 constant_dynamic-update-slice_fusion.6
  357.2 6.6 cholesky.156
  369.4 21.5 %custom-call.22 = f32[2,128,128]{1,2,0:T(8,128)} custom-call(f32[2,128,128]{2,1,0:T(8,128)} %pad_maximum_fusion.5), custom_call_target="InvertDiagBlocksLowerTriangular" | custom-call | tf_op jit(solution)/shard_map/triangular_solve/custom-call.4 | solution.py:36
  390.9 1.7 copy.14
  402.3 1.6 select_reduce_fusion.1
  417.2 2.2 fusion.100
  421.2 7.0 fusion.4
  428.2 2.2 fusion.6
  430.4 2.5 convolution_subtract_fusion.1
  434.5 68.8 %all-reduce.18.cloned.1.call-done = f32[2048,192]{0,1:T(8,128)} async-done(((f32[2048,192]{0,1:T(8,128)}), f32[2048,192]{0,1:T(8,128)}) %all-reduce.18.cloned.1.call-update) | async-done | bytes 1572880 | tf_op jit(solution)/shard_map/psum | solution.py:14
  503.4 40.5 %convolution_bitcast_fusion = f32[4096,192]{0,1:T(8,128)S(1)} fusion(f32[2048,192]{0,1:T(8,128)} %all-reduce.18.cloned.1.call-done, f32[4096,2048]{1,0:T(8,128)} %param.11), kind=kOutput, calls=%fused_computation.2 | convolution fusion | flops 19327352832 | bytes 38273024 | tf_op jit(solution)/shard_map/dot_general | solution.py:18
  543.9 37.6 %convolution_bitcast_fusion.1 = f32[4096,192]{0,1:T(8,128)S(1)} fusion(f32[2048,192]{0,1:T(8,128)S(1)} %copy-done.3, f32[4096,2048]{1,0:T(8,128)} %param.10), kind=kOutput, calls=%fused_computation.3 | convolution fusion | flops 19327352832 | bytes 38273024 | tf_op jit(solution)/shard_map/dot_general | solution.py:18
  581.4 3.1 pad_maximum_fusion.1
  584.6 103.2 %all-reduce.20.cloned.1.call-done = f32[4096,384]{0,1:T(8,128)} async-done(((f32[4096,384]{0,1:T(8,128)}), f32[4096,384]{0,1:T(8,128)}) %all-reduce.20.cloned.1.call-update) | async-done | bytes 6291472 | tf_op jit(solution)/shard_map/psum | solution.py:52
  687.8 9.3 %fusion.101 = f32[192,384]{1,0:T(8,128)} fusion(f32[4096,384]{0,1:T(8,128)} %all-reduce.20.cloned.1.call-done, f32[4096,64]{0,1:T(8,128)S(1)} %fusion.8, f32[4096,64]{0,1:T(8,128)S(1)} %convolution_subtract_fusion.1, f32[4096,64]{0,1:T(8,128)S(1)} %copy-done.1), kind=kOutput, calls=%fused_computation.190 | convolution fusion | flops 3625451520 | bytes 9732096 | tf_op jit(solution)/shard_map/dot_general | solution.py:18
  697.1 36.2 %all-reduce.22.cloned.1.call-done = f32[192,384]{1,0:T(8,128)} async-done(((f32[192,384]{1,0:T(8,128)}), f32[192,384]{1,0:T(8,128)}) %all-reduce.22.cloned.1.call-update) | async-done | bytes 294928 | tf_op jit(solution)/shard_map/psum | solution.py:55
  733.3 1.8 slice.248
  735.1 1.7 copy.18
  736.8 1.9 bitcast_add_fusion.3
  738.8 1.7 copy.19
  740.5 1.6 broadcast_multiply_fusion
  742.1 1.7 copy.20
  746.2 13.2 %cholesky.174 = f32[128,128]{1,0:T(8,128)} custom-call(f32[128,128]{1,0:T(8,128)} %cholesky.211), custom_call_target="Cholesky" | custom-call | tf_op jit(solution)/shard_map/jit(cholesky)/cholesky | solution.py:24
  762.4 11.3 %custom-call.23 = f32[1,128,128]{1,2,0:T(8,128)} custom-call(f32[1,128,128]{2,1,0:T(8,128)} %get-tuple-element.79), custom_call_target="InvertDiagBlocksLowerTriangular" | custom-call | tf_op jit(solution)/shard_map/jit(cholesky)/cholesky | solution.py:24
  773.6 1.7 constant_dynamic-update-slice_fusion.4
  776.8 6.6 cholesky.194
  789.0 21.3 %custom-call.26 = f32[2,128,128]{1,2,0:T(8,128)} custom-call(f32[2,128,128]{2,1,0:T(8,128)} %pad_maximum_fusion.6), custom_call_target="InvertDiagBlocksLowerTriangular" | custom-call | tf_op jit(solution)/shard_map/triangular_solve/custom-call.4 | solution.py:36
  810.3 1.7 copy.21
  821.1 1.6 select_reduce_fusion
  836.0 3.1 fusion.99
  839.2 2.7 fusion.12
  842.2 7.0 fusion
  849.1 2.2 fusion.2
  851.3 3.5 convolution_subtract_fusion
  (159 shorter events, 75.5 us)
Async XLA Ops:
  7.2 77.1 %all-reduce.12.cloned.1.call-start = ((), (), s32[]{:S(2)}) async-start(), calls=%async_computation | async-start | bytes 3145728 | tf_op jit(solution)/shard_map/psum | solution.py:14
  12.5 256.0 %all-reduce.14.cloned.1.call-start = ((), (), s32[]{:S(2)}) async-start(), calls=%async_computation.1 | async-start | bytes 12582912 | tf_op jit(solution)/shard_map/psum | solution.py:52
  84.3 40.1 %copy-start.2 = (f32[2048,192]{0,1:T(8,128)S(1)}, f32[2048,192]{0,1:T(8,128)}, u32[]{:S(2)}) copy-start(f32[2048,192]{0,1:T(8,128)} %all-reduce.12.cloned.1.call-done) | copy-start | bytes 4718596
  165.3 148.6 %all-reduce.16.cloned.1.call-start = ((), (), s32[]{:S(2)}) async-start(), calls=%async_computation.2 | async-start | bytes 589824 | tf_op jit(solution)/shard_map/psum | solution.py:55
  277.7 225.6 %all-reduce.18.cloned.1.call-start = ((), (), s32[]{:S(2)}) async-start(), calls=%async_computation.3 | async-start | bytes 3145728 | tf_op jit(solution)/shard_map/psum | solution.py:14
  313.9 78.7 %copy-start.6 = (f32[192,384]{1,0:T(8,128)S(1)}, f32[192,384]{1,0:T(8,128)}, u32[]{:S(2)}) copy-start(f32[192,384]{1,0:T(8,128)} %all-reduce.16.cloned.1.call-done) | copy-start | bytes 884740
  322.1 0.7 copy-start.14
  368.0 0.7 copy-start.9
  396.7 0.7 copy-start.10
  400.9 0.6 copy-start.15
  408.8 6.5 copy-start.13
  412.3 8.9 %slice-start = ((s8[6291456]{0:T(1024)(128)(4,1)}), s8[4194304]{0:T(1024)(128)(4,1)S(1)}, s32[]{:S(2)}) async-start(s8[6291456]{0:T(1024)(128)(4,1)} %bitcast.196), calls=%async_computation.6 | async-start | bytes 8388608
  414.1 5.6 copy-start.4
  414.1 5.6 copy-start.5
  417.2 4.0 slice-start.1
  419.4 13.5 %copy-start = (f32[4096,64]{0,1:T(8,128)}, f32[4096,64]{0,1:T(8,128)S(1)}, u32[]{:S(2)}) copy-start(f32[4096,64]{0,1:T(8,128)S(1)} %fusion.100) | copy-start | bytes 3145732
  434.5 253.3 %all-reduce.20.cloned.1.call-start = ((), (), s32[]{:S(2)}) async-start(), calls=%async_computation.4 | async-start | bytes 12582912 | tf_op jit(solution)/shard_map/psum | solution.py:52
  503.4 40.5 %copy-start.3 = (f32[2048,192]{0,1:T(8,128)S(1)}, f32[2048,192]{0,1:T(8,128)}, u32[]{:S(2)}) copy-start(f32[2048,192]{0,1:T(8,128)} %all-reduce.18.cloned.1.call-done) | copy-start | bytes 4718596
  584.5 103.3 %copy-start.1 = (f32[4096,64]{0,1:T(8,128)S(1)}, f32[4096,64]{0,1:T(8,128)}, u32[]{:S(2)}) copy-start(f32[4096,64]{0,1:T(8,128)} %copy-done) | copy-start | bytes 3145732
  584.5 148.8 %all-reduce.22.cloned.1.call-start = ((), (), s32[]{:S(2)}) async-start(), calls=%async_computation.5 | async-start | bytes 589824 | tf_op jit(solution)/shard_map/psum | solution.py:55
  733.3 78.7 %copy-start.7 = (f32[192,384]{1,0:T(8,128)S(1)}, f32[192,384]{1,0:T(8,128)}, u32[]{:S(2)}) copy-start(f32[192,384]{1,0:T(8,128)} %all-reduce.22.cloned.1.call-done) | copy-start | bytes 884740
  744.9 0.7 copy-start.16
  787.6 0.7 copy-start.8
  816.1 0.7 copy-start.11
  827.6 6.4 copy-start.12
  831.1 11.0 %slice-start.2 = ((s8[6291456]{0:T(1024)(128)(4,1)}), s8[4194304]{0:T(1024)(128)(4,1)S(1)}, s32[]{:S(2)}) async-start(s8[6291456]{0:T(1024)(128)(4,1)} %bitcast.198), calls=%async_computation.8 | async-start | bytes 8388608
  836.0 6.1 slice-start.3
Sparse Core Ops, SparseCore 0:
  12.6 71.6 all-reduce.11
  165.4 103.0 all-reduce.13
  277.8 36.0 all-reduce.15
  434.6 68.7 all-reduce.17
  584.7 103.0 all-reduce.19
  697.3 36.0 all-reduce.21
where the time goes:
time: 870 us; the launch traced here: 862 us
  waiting for transfers between devices  419 us (48%)
  matrix products  251 us (29%)
  other arithmetic  138 us (16%)
  local copies, waits for them, and re-layouts  33.3 us (4%)
  between operations  20.3 us (2%)
    dot_general x52, matrix products, matmul(): jnp.dot(left, right, precision=lax.Precision.HIGHEST, preferred_element_t...  228 us
    psum x2, waiting for transfers between devices, local(): lax.psum(jnp.concatenate([matmul(a_matrix, matched), matmul(b_matrix, mat...  206 us
    psum x2, waiting for transfers between devices, spread(): return lax.psum(kept, axis)  141 us
    psum x2, waiting for transfers between devices, local(): grams = lax.psum(matmul(panel.T, products), 'row')  72.1 us
    another operation x14, other arithmetic, ritz_step(): lower = jnp.linalg.cholesky(gram_b)  68.9 us
    another operation x10, other arithmetic, ritz_step(): lax.linalg.triangular_solve(lower, filtered, left_side=True, lower=True,...  46.2 us
  transfers between devices with their start and end apart: 6, of which 6 were waited for; matrix products, arithmetic and copies ran while one was open for 0% of the time, Pallas kernels for 0%

commit v1 on v0

--- a/solution.py
+++ b/solution.py
@@ -52,7 +52,7 @@
         products = lax.psum(
             jnp.concatenate([matmul(a_matrix, matched), matmul(b_matrix, matched)], axis=1), "col"
         )
-        grams = lax.psum(matmul(panel.T, products), "row")
+        grams = jnp.sum(lax.all_gather(matmul(panel.T, products), "row"), axis=0)
         coords, reduced = ritz_step(grams[:, : 3 * width], grams[:, 3 * width :], width)
         new_resid = matmul(products[:, : 3 * width], coords) - matmul(
             matmul(products[:, 3 * width :], coords), reduced

time: 870 us -> 858 us (0.986)
  waiting for transfers between devices: 419 us -> 407 us
    psum x2 -> x0, waiting for transfers between devices: 72.1 us -> none  [local(): grams = lax.psum(matmul(panel.T, products), 'row')]
    all_gather x0 -> x2, waiting for transfers between devices: none -> 60.7 us  [local(): grams = jnp.sum(lax.all_gather(matmul(panel.T, products), 'row'), axis=0)]
where the time goes in v1:
time: 858 us; the launch traced here: 850 us
  waiting for transfers between devices  407 us (47%)
  matrix products  251 us (29%)
  other arithmetic  140 us (16%)
  local copies, waits for them, and re-layouts  31.3 us (4%)
  between operations  20.1 us (2%)
    dot_general x52, matrix products, matmul(): jnp.dot(left, right, precision=lax.Precision.HIGHEST, preferred_element_t...  228 us
    psum x2, waiting for transfers between devices, local(): lax.psum(jnp.concatenate([matmul(a_matrix, matched), matmul(b_matrix, mat...  206 us
    psum x2, waiting for transfers between devices, spread(): return lax.psum(kept, axis)  140 us
    another operation x14, other arithmetic, ritz_step(): lower = jnp.linalg.cholesky(gram_b)  68.8 us
    all_gather x2, waiting for transfers between devices, local(): grams = jnp.sum(lax.all_gather(matmul(panel.T, products), 'row'), axis=0)  60.7 us
    another operation x10, other arithmetic, ritz_step(): lax.linalg.triangular_solve(lower, filtered, left_side=True, lower=True,...  46.2 us
  transfers between devices with their start and end apart: 6, of which 6 were waited for; matrix products, arithmetic and copies ran while one was open for 0% of the time, Pallas kernels for 0%

profile of v1, /device:TPU:0, one launch (start us, length us, event | category | flops | bytes accessed | tf_op | source)
XLA Modules:
  0.0 850.0 jit_solution(4971815525246599657)
XLA Ops:
  12.5 71.8 %all-reduce.10.cloned.1.call-done = f32[2048,192]{0,1:T(8,128)} async-done(((f32[2048,192]{0,1:T(8,128)}), f32[2048,192]{0,1:T(8,128)}) %all-reduce.10.cloned.1.call-update) | async-done | bytes 1572880 | tf_op jit(solution)/shard_map/psum | solution.py:14
  84.3 40.1 %convolution_bitcast_fusion.2 = f32[4096,192]{0,1:T(8,128)S(1)} fusion(f32[2048,192]{0,1:T(8,128)} %all-reduce.10.cloned.1.call-done, f32[4096,2048]{1,0:T(8,128)} %param.11), kind=kOutput, calls=%fused_computation.4 | convolution fusion | flops 19327352832 | bytes 38273024 | tf_op jit(solution)/shard_map/dot_general | solution.py:18
  124.4 37.8 %convolution_bitcast_fusion.3 = f32[4096,192]{0,1:T(8,128)S(1)} fusion(f32[2048,192]{0,1:T(8,128)S(1)} %copy-done.2, f32[4096,2048]{1,0:T(8,128)} %param.10), kind=kOutput, calls=%fused_computation.5 | convolution fusion | flops 19327352832 | bytes 38273024 | tf_op jit(solution)/shard_map/dot_general | solution.py:18
  162.2 3.1 pad_maximum_fusion
  165.3 103.2 %all-reduce.12.cloned.1.call-done = f32[4096,384]{0,1:T(8,128)} async-done(((f32[4096,384]{0,1:T(8,128)}), f32[4096,384]{0,1:T(8,128)}) %all-reduce.12.cloned.1.call-update) | async-done | bytes 6291472 | tf_op jit(solution)/shard_map/psum | solution.py:52
  268.5 9.2 %fusion.104 = f32[192,384]{1,0:T(8,128)} fusion(f32[4096,192]{0,1:T(8,128)S(1)} %constant_dynamic-update-slice_fusion, f32[4096,384]{0,1:T(8,128)} %all-reduce.12.cloned.1.call-done), kind=kOutput, calls=%fused_computation.191 | convolution fusion | flops 3623878656 | bytes 9732096 | tf_op jit(solution)/shard_map/dot_general | solution.py:18
  278.0 30.2 %all-gather.5.cloned.1.call-done = f32[768,384]{1,0:T(8,128)} async-done(((f32[192,384]{1,0:T(8,128)}), f32[768,384]{1,0:T(8,128)}) %all-gather.5.cloned.1.call-update) | async-done | bytes 1179664 | tf_op jit(solution)/shard_map/all_gather | solution.py:55
  310.4 1.7 copy.8
  312.1 1.7 fusion.42
  313.8 1.7 copy.10
  317.9 1.6 copy.11
  319.5 13.2 %cholesky.136 = f32[128,128]{1,0:T(8,128)} custom-call(f32[128,128]{1,0:T(8,128)} %copy.11), custom_call_target="Cholesky" | custom-call | tf_op jit(solution)/shard_map/jit(cholesky)/cholesky | solution.py:24
  335.6 11.3 %custom-call.19 = f32[1,128,128]{1,2,0:T(8,128)} custom-call(f32[1,128,128]{2,1,0:T(8,128)} %get-tuple-element.81), custom_call_target="InvertDiagBlocksLowerTriangular" | custom-call | tf_op jit(solution)/shard_map/jit(cholesky)/cholesky | solution.py:24
  346.9 1.8 constant_dynamic-update-slice_fusion.6
  348.7 1.5 convolution_subtract_fusion.9
  351.7 6.6 cholesky.156
  363.8 21.5 %custom-call.22 = f32[2,128,128]{1,2,0:T(8,128)} custom-call(f32[2,128,128]{2,1,0:T(8,128)} %pad_maximum_fusion.5), custom_call_target="InvertDiagBlocksLowerTriangular" | custom-call | tf_op jit(solution)/shard_map/triangular_solve/custom-call.4 | solution.py:36
  385.3 1.7 copy.14
  396.7 1.5 select_reduce_fusion.1
  411.5 2.2 fusion.100
  415.5 7.0 fusion.4
  422.5 2.2 fusion.6
  424.7 2.5 convolution_subtract_fusion.1
  428.8 68.3 %all-reduce.14.cloned.1.call-done = f32[2048,192]{0,1:T(8,128)} async-done(((f32[2048,192]{0,1:T(8,128)}), f32[2048,192]{0,1:T(8,128)}) %all-reduce.14.cloned.1.call-update) | async-done | bytes 1572880 | tf_op jit(solution)/shard_map/psum | solution.py:14
  497.1 40.5 %convolution_bitcast_fusion = f32[4096,192]{0,1:T(8,128)S(1)} fusion(f32[2048,192]{0,1:T(8,128)} %all-reduce.14.cloned.1.call-done, f32[4096,2048]{1,0:T(8,128)} %param.11), kind=kOutput, calls=%fused_computation.2 | convolution fusion | flops 19327352832 | bytes 38273024 | tf_op jit(solution)/shard_map/dot_general | solution.py:18
  537.6 37.6 %convolution_bitcast_fusion.1 = f32[4096,192]{0,1:T(8,128)S(1)} fusion(f32[2048,192]{0,1:T(8,128)S(1)} %copy-done.3, f32[4096,2048]{1,0:T(8,128)} %param.10), kind=kOutput, calls=%fused_computation.3 | convolution fusion | flops 19327352832 | bytes 38273024 | tf_op jit(solution)/shard_map/dot_general | solution.py:18
  575.2 3.1 pad_maximum_fusion.1
  578.3 103.2 %all-reduce.16.cloned.1.call-done = f32[4096,384]{0,1:T(8,128)} async-done(((f32[4096,384]{0,1:T(8,128)}), f32[4096,384]{0,1:T(8,128)}) %all-reduce.16.cloned.1.call-update) | async-done | bytes 6291472 | tf_op jit(solution)/shard_map/psum | solution.py:52
  681.5 9.4 %fusion.101 = f32[192,384]{1,0:T(8,128)} fusion(f32[4096,384]{0,1:T(8,128)} %all-reduce.16.cloned.1.call-done, f32[4096,64]{0,1:T(8,128)S(1)} %fusion.8, f32[4096,64]{0,1:T(8,128)S(1)} %convolution_subtract_fusion.1, f32[4096,64]{0,1:T(8,128)S(1)} %copy-done.1), kind=kOutput, calls=%fused_computation.190 | convolution fusion | flops 3625451520 | bytes 9732096 | tf_op jit(solution)/shard_map/dot_general | solution.py:18
  690.9 30.5 %all-gather.7.cloned.1.call-done = f32[768,384]{1,0:T(8,128)} async-done(((f32[192,384]{1,0:T(8,128)}), f32[768,384]{1,0:T(8,128)}) %all-gather.7.cloned.1.call-update) | async-done | bytes 1179664 | tf_op jit(solution)/shard_map/all_gather | solution.py:55
  723.6 1.7 copy.18
  725.3 1.7 bitcast_add_fusion.3
  727.0 1.7 copy.19
  728.7 1.6 broadcast_multiply_fusion
  730.3 1.7 copy.20
  734.4 13.2 %cholesky.174 = f32[128,128]{1,0:T(8,128)} custom-call(f32[128,128]{1,0:T(8,128)} %cholesky.211), custom_call_target="Cholesky" | custom-call | tf_op jit(solution)/shard_map/jit(cholesky)/cholesky | solution.py:24
  750.6 11.3 %custom-call.23 = f32[1,128,128]{1,2,0:T(8,128)} custom-call(f32[1,128,128]{2,1,0:T(8,128)} %get-tuple-element.79), custom_call_target="InvertDiagBlocksLowerTriangular" | custom-call | tf_op jit(solution)/shard_map/jit(cholesky)/cholesky | solution.py:24
  761.9 1.7 constant_dynamic-update-slice_fusion.4
  763.5 1.5 convolution_subtract_fusion.7
  765.1 6.6 cholesky.194
  777.2 21.3 %custom-call.26 = f32[2,128,128]{1,2,0:T(8,128)} custom-call(f32[2,128,128]{2,1,0:T(8,128)} %pad_maximum_fusion.6), custom_call_target="InvertDiagBlocksLowerTriangular" | custom-call | tf_op jit(solution)/shard_map/triangular_solve/custom-call.4 | solution.py:36
  798.5 1.7 copy.21
  809.3 1.6 select_reduce_fusion
  824.2 3.1 fusion.99
  827.3 2.7 fusion.12
  830.3 7.0 fusion
  837.3 2.2 fusion.2
  839.5 3.5 convolution_subtract_fusion
  (157 shorter events, 76.6 us)
Async XLA Ops:
  7.2 77.1 %all-reduce.10.cloned.1.call-start = ((), (), s32[]{:S(2)}) async-start(), calls=%async_computation | async-start | bytes 3145728 | tf_op jit(solution)/shard_map/psum | solution.py:14
  12.5 256.0 %all-reduce.12.cloned.1.call-start = ((), (), s32[]{:S(2)}) async-start(), calls=%async_computation.1 | async-start | bytes 12582912 | tf_op jit(solution)/shard_map/psum | solution.py:52
  84.3 40.1 %copy-start.2 = (f32[2048,192]{0,1:T(8,128)S(1)}, f32[2048,192]{0,1:T(8,128)}, u32[]{:S(2)}) copy-start(f32[2048,192]{0,1:T(8,128)} %all-reduce.10.cloned.1.call-done) | copy-start | bytes 4718596
  165.2 143.0 %all-gather.5.cloned.1.call-start = ((), (), s32[]{:S(2)}) async-start(), calls=%async_computation.4 | async-start | bytes 1474560 | tf_op jit(solution)/shard_map/all_gather | solution.py:55
  277.7 219.4 %all-reduce.14.cloned.1.call-start = ((), (), s32[]{:S(2)}) async-start(), calls=%async_computation.2 | async-start | bytes 3145728 | tf_op jit(solution)/shard_map/psum | solution.py:14
  316.6 0.7 copy-start.12
  362.4 0.7 copy-start.7
  391.1 0.7 copy-start.8
  395.3 0.6 copy-start.13
  403.1 6.5 copy-start.11
  406.6 8.9 %slice-start = ((s8[6291456]{0:T(1024)(128)(4,1)}), s8[4194304]{0:T(1024)(128)(4,1)S(1)}, s32[]{:S(2)}) async-start(s8[6291456]{0:T(1024)(128)(4,1)} %bitcast.198), calls=%async_computation.6 | async-start | bytes 8388608
  408.3 5.6 copy-start.4
  408.4 5.6 copy-start.5
  411.5 4.0 slice-start.1
  413.7 13.5 %copy-start = (f32[4096,64]{0,1:T(8,128)}, f32[4096,64]{0,1:T(8,128)S(1)}, u32[]{:S(2)}) copy-start(f32[4096,64]{0,1:T(8,128)S(1)} %fusion.100) | copy-start | bytes 3145732
  428.8 252.7 %all-reduce.16.cloned.1.call-start = ((), (), s32[]{:S(2)}) async-start(), calls=%async_computation.3 | async-start | bytes 12582912 | tf_op jit(solution)/shard_map/psum | solution.py:52
  497.1 40.5 %copy-start.3 = (f32[2048,192]{0,1:T(8,128)S(1)}, f32[2048,192]{0,1:T(8,128)}, u32[]{:S(2)}) copy-start(f32[2048,192]{0,1:T(8,128)} %all-reduce.14.cloned.1.call-done) | copy-start | bytes 4718596
  578.2 103.3 %copy-start.1 = (f32[4096,64]{0,1:T(8,128)S(1)}, f32[4096,64]{0,1:T(8,128)}, u32[]{:S(2)}) copy-start(f32[4096,64]{0,1:T(8,128)} %copy-done) | copy-start | bytes 3145732
  578.3 143.1 %all-gather.7.cloned.1.call-start = ((), (), s32[]{:S(2)}) async-start(), calls=%async_computation.5 | async-start | bytes 1474560 | tf_op jit(solution)/shard_map/all_gather | solution.py:55
  733.1 0.7 copy-start.14
  775.8 0.7 copy-start.6
  804.3 0.7 copy-start.9
  815.8 6.4 copy-start.10
  819.3 11.0 %slice-start.2 = ((s8[6291456]{0:T(1024)(128)(4,1)}), s8[4194304]{0:T(1024)(128)(4,1)S(1)}, s32[]{:S(2)}) async-start(s8[6291456]{0:T(1024)(128)(4,1)} %bitcast.200), calls=%async_computation.8 | async-start | bytes 8388608
  824.2 6.1 slice-start.3
Sparse Core Ops, SparseCore 0:
  12.6 71.6 all-reduce.9
  165.4 103.0 all-reduce.11
  277.8 30.3 all-gather.4
  428.9 68.1 all-reduce.13
  578.4 103.0 all-reduce.15
  691.0 30.3 all-gather.6
